TPU v7x, 256 devices: a whole 4x4x8 slice. The times are simulated.
256 devices in a mesh: ctx: 32 (over z_hi, x, core), tp: 8 (over y, z_lo).
Axes of the slice: x: 4, y: 4, z: 8 (z_hi: 4, z_lo: 2; z = z_hi * 2 + z_lo), core: 2. Of those that a mesh axis runs over, the one named last changes fastest.
Arguments:
- features: bfloat16 [16384, 3, 4096], P('ctx', None, 'tp'), may hold values from -6 to 6
- short_filter: float32 [3, 7, 4096], P(None, None, 'tp'), may hold values from -2 to 2
- decay_rate: float32 [16, 4096], P(None, 'tp'), may hold values from 0 to 1, as said below
- residue: float32 [16, 4096], P(None, 'tp'), may hold values from -2 to 2
- skip_gain: float32 [4096], P('tp'), may hold values from -4 to 4
- norm_gain: float32 [4096], replicated, may hold values from 0.1 to 1.9
- qkv_weight: bfloat16 [4096, 3, 2048], P('ctx', None, 'tp'), may hold values from -2 to 2
Outputs:
- mixer: bfloat16 [16384, 4096], P('ctx', 'tp')
- attended: bfloat16 [16384, 2048], P('ctx', 'tp')
Inputs may be any that keep to these rules, and one draw needn't show every extreme that they name: `decay_rate`: decay rates are positive.
All inputs are finite; a program needn't handle non-finite values.
Results may differ from a plain program's by a relative error of at most 0.01.
Values may be sent and summed in bfloat16 or wider, within the bound.
No kernel may reach another device: no remote copies, remote signals or barrier semaphores. Data moves between devices by JAX's collectives and lax.ppermute only.
A program may use at most 128 MiB of HBM per device.

v0:
```python
from functools import reduce
import math
import jax
import jax.numpy as jnp
from jax import lax
from jax.sharding import PartitionSpec as P

HD = 128
TAPS = 7
WINDOW = 3
EPSILON = 1e-06
PRECISE = lax.Precision.HIGHEST


def from_behind(value, axis, steps):
    count = lax.axis_size(axis)
    leading, last = (max(0, -steps), min(count, count - steps))
    return lax.ppermute(value, axis, [(source, source + steps) for source in range(leading, last)])


def modal_toeplitz(mixing, decay, block_len):
    distance = jnp.arange(block_len)[:, None] - jnp.arange(block_len)[None, :]
    lag_float = jnp.maximum(distance, 0).astype(jnp.float32)
    channels = mixing.shape[1]
    start = jnp.zeros((channels, block_len, block_len), jnp.float32)

    def add_mode(mode, running):
        weight_row = lax.dynamic_index_in_dim(mixing, mode, 0, keepdims=False)
        rate_row = lax.dynamic_index_in_dim(decay, mode, 0, keepdims=False)
        term = weight_row[:, None, None] * jnp.exp(-rate_row[:, None, None] * lag_float[None])
        return running + term

    summed = lax.fori_loop(0, mixing.shape[0], add_mode, start)
    return jnp.where(distance[None] >= 0, summed, 0.0)


def channel_conv(signal, decay, residue, skip_gain):
    channels, length = signal.shape
    block_len = math.gcd(length, 256)
    block_count = length // block_len
    blocked = signal.reshape(channels, block_count, block_len)
    rate_cols = decay.T
    mode_weights = residue * jnp.sqrt(decay)
    mixing = mode_weights.T
    offsets = jnp.arange(block_len).astype(jnp.float32)
    trailing = jnp.exp(-rate_cols[:, :, None] * (block_len - 1.0 - offsets)[None, None, :])
    block_ends = jnp.einsum("cbs,cns->cnb", blocked, trailing, precision=PRECISE)
    block_ids = jnp.arange(block_count)
    spacing = block_ids[:, None] - 1 - block_ids[None, :]
    powers = (block_len * jnp.maximum(spacing, 0)).astype(jnp.float32)
    carry = jnp.where(
        spacing[None, None] >= 0, jnp.exp(-rate_cols[:, :, None, None] * powers[None, None]), 0.0
    )
    entering = jnp.einsum("cnkb,cnb->cnk", carry, block_ends, precision=PRECISE)
    leading = jnp.exp(-rate_cols[:, :, None] * (offsets + 1.0)[None, None, :])
    across = jnp.einsum("cnk,cns->cks", entering * mixing[:, :, None], leading, precision=PRECISE)
    toeplitz = modal_toeplitz(mode_weights, decay, block_len)
    within = jnp.einsum("cts,cbs->cbt", toeplitz, blocked, precision=PRECISE)
    return (within + across + skip_gain[:, None, None] * blocked).reshape(channels, length)


def on_device(features, short_filter, decay_rate, residue, skip_gain, norm_gain, qkv_weight):
    tok_dev, _, channels = features.shape
    rim_rows = features[tok_dev - (TAPS - 1) :]
    before = from_behind(rim_rows, "ctx", 1)
    extended = jnp.concatenate([before, features], axis=0).astype(jnp.float32)
    short_conv = jnp.zeros((tok_dev, 3, channels), jnp.float32)
    for offset in range(TAPS):
        first_row = TAPS - 1 - offset
        short_conv = (
            short_conv
            + short_filter[:, offset, :][None] * extended[first_row : first_row + tok_dev]
        )
    gated = (short_conv[:, 1] * short_conv[:, 2]).astype(jnp.bfloat16)
    per_device = channels // lax.axis_size("ctx")
    by_channel = lax.all_to_all(gated.T, "ctx", split_axis=0, concat_axis=1, tiled=True)
    first_channel = lax.axis_index("ctx") * per_device
    decay_part = lax.dynamic_slice_in_dim(decay_rate, first_channel, per_device, 1)
    residue_part = lax.dynamic_slice_in_dim(residue, first_channel, per_device, 1)
    skip_part = lax.dynamic_slice_in_dim(skip_gain, first_channel, per_device, 0)
    filtered = channel_conv(
        by_channel.astype(jnp.float32), decay_part, residue_part, skip_part
    ).astype(jnp.bfloat16)
    long_part = lax.all_to_all(filtered, "ctx", split_axis=1, concat_axis=0, tiled=True).T
    mixer = (short_conv[:, 0] * long_part.astype(jnp.float32)).astype(jnp.bfloat16)
    gathered = lax.all_gather(mixer, "tp", axis=1, tiled=True)
    as_float = gathered.astype(jnp.float32)
    inverse = lax.rsqrt(jnp.mean(as_float * as_float, axis=1, keepdims=True) + EPSILON)
    normed = (as_float * inverse * norm_gain[None]).astype(jnp.bfloat16)
    head_cols = qkv_weight.shape[2]
    shard_rows = lax.all_gather(qkv_weight, "ctx", axis=0, tiled=True)
    flat_rows = shard_rows.reshape(shard_rows.shape[0], 3 * head_cols)
    projected = jnp.dot(normed, flat_rows, preferred_element_type=jnp.float32).astype(jnp.bfloat16)
    heads = head_cols // HD
    query = projected[:, :head_cols].reshape(tok_dev, heads, HD)
    kv_pair = projected[:, head_cols:]
    blocks_kv = [kv_pair]
    for lag_step in range(WINDOW - 1):
        blocks_kv.append(from_behind(blocks_kv[-1], "ctx", 1))
    position = lax.axis_index("ctx")
    row_ids = jnp.arange(tok_dev)
    causal = row_ids[:, None] >= row_ids[None, :]
    score_list = []
    for lag_step in range(WINDOW):
        keys = blocks_kv[lag_step][:, :head_cols].reshape(tok_dev, heads, HD)
        scores = jnp.einsum(
            "thd,shd->hts", query, keys, preferred_element_type=jnp.float32
        ) / math.sqrt(HD)
        if lag_step == 0:
            allowed = causal
        else:
            allowed = jnp.broadcast_to(position >= lag_step, causal.shape)
        score_list.append(jnp.where(allowed[None], scores, -jnp.inf))
    peak = reduce(jnp.maximum, [jnp.max(entry, axis=2) for entry in score_list])
    total = jnp.zeros((heads, tok_dev), jnp.float32)
    output = jnp.zeros((tok_dev, heads, HD), jnp.float32)
    for lag_step in range(WINDOW):
        expo = jnp.exp(score_list[lag_step] - peak[:, :, None])
        total = total + jnp.sum(expo, axis=2)
        values = blocks_kv[lag_step][:, head_cols:].reshape(tok_dev, heads, HD)
        output = output + jnp.einsum(
            "hts,shd->thd", expo.astype(jnp.bfloat16), values, preferred_element_type=jnp.float32
        )
    attended = (output / total.T[:, :, None]).astype(jnp.bfloat16).reshape(tok_dev, head_cols)
    return (mixer, attended)


def solution(mesh):
    placed = (
        P("ctx", None, "tp"),
        P(None, None, "tp"),
        P(None, "tp"),
        P(None, "tp"),
        P("tp"),
        P(),
        P("ctx", None, "tp"),
    )
    return jax.shard_map(
        on_device,
        mesh=mesh,
        in_specs=placed,
        out_specs=(P("ctx", "tp"), P("ctx", "tp")),
        check_vma=False,
    )
```

profile of v0, /device:TPU:128, one launch (start us, length us, event | category | flops | bytes accessed | tf_op | source)
XLA Modules:
  0.0 409.7 jit_solution(15432068327113039703)
XLA Ops:
  7.2 0.7 slice.81
  7.9 1.0 copy.27
  8.9 1.9 collective-permute-start
  10.8 1.8 fusion.108
  12.6 0.8 sqrt_multiply_fusion
  13.4 79.2 %while.14 = (s32[]{:T(128)}, f32[16,256,256]{2,1,0:T(8,128)}, f32[16,16]{1,0:T(8,128)S(1)}, f32[16,16]{1,0:T(8,128)S(1)}, s32[]{:T(128)}, /*index=5*/s32[]{:T(128)}) while((s32[]{:T(128)}, f32[16,256,256]{2,1,0:T(8,128)}, f32[16,16]{1,0:T(8,128)S(1)}, f32[16,16]{1,0:T(8,128)S(1)}, s32[]{:T(128)}, /*index=5*/s32[]{:T(128)}) %tuple.60), condition=%wide.region_1.2_spmd.clone, body=%wide.region_0.1_spmd.clone.sunk | while | flops 4390931 | bytes 8913363 | solution.py:33
  13.5 2.9 select_add_fusion.2
  16.4 5.0 %select_add_fusion.2 = f32[16,256,256]{2,1,0:T(8,128)} fusion(f32[16,256,256]{2,1,0:T(8,128)} %get-tuple-element.195, f32[256,256]{1,0:T(8,128)S(1)} %maximum_convert_fusion.3, f32[16]{0:T(128)S(1)} %get-tuple-element.186, f32[16]{0:T(128)S(1)} %get-tuple-element.187, pred[]{:T(512)S(6)} %compare.3), kind=kLoop, calls=%fused_computation.1.clone.1 | loop fusion | flops 4194304 | bytes 8650881 | tf_op jit(solution)/shard_map/while/body/eval_jaxpr/add | solution.py:31
  21.5 5.0 %select_add_fusion.2 = f32[16,256,256]{2,1,0:T(8,128)} fusion(f32[16,256,256]{2,1,0:T(8,128)} %get-tuple-element.195, f32[256,256]{1,0:T(8,128)S(1)} %maximum_convert_fusion.3, f32[16]{0:T(128)S(1)} %get-tuple-element.186, f32[16]{0:T(128)S(1)} %get-tuple-element.187, pred[]{:T(512)S(6)} %compare.3), kind=kLoop, calls=%fused_computation.1.clone.1 | loop fusion | flops 4194304 | bytes 8650881 | tf_op jit(solution)/shard_map/while/body/eval_jaxpr/add | solution.py:31
  26.5 5.0 %select_add_fusion.2 = f32[16,256,256]{2,1,0:T(8,128)} fusion(f32[16,256,256]{2,1,0:T(8,128)} %get-tuple-element.195, f32[256,256]{1,0:T(8,128)S(1)} %maximum_convert_fusion.3, f32[16]{0:T(128)S(1)} %get-tuple-element.186, f32[16]{0:T(128)S(1)} %get-tuple-element.187, pred[]{:T(512)S(6)} %compare.3), kind=kLoop, calls=%fused_computation.1.clone.1 | loop fusion | flops 4194304 | bytes 8650881 | tf_op jit(solution)/shard_map/while/body/eval_jaxpr/add | solution.py:31
  31.6 5.0 %select_add_fusion.2 = f32[16,256,256]{2,1,0:T(8,128)} fusion(f32[16,256,256]{2,1,0:T(8,128)} %get-tuple-element.195, f32[256,256]{1,0:T(8,128)S(1)} %maximum_convert_fusion.3, f32[16]{0:T(128)S(1)} %get-tuple-element.186, f32[16]{0:T(128)S(1)} %get-tuple-element.187, pred[]{:T(512)S(6)} %compare.3), kind=kLoop, calls=%fused_computation.1.clone.1 | loop fusion | flops 4194304 | bytes 8650881 | tf_op jit(solution)/shard_map/while/body/eval_jaxpr/add | solution.py:31
  36.7 5.0 %select_add_fusion.2 = f32[16,256,256]{2,1,0:T(8,128)} fusion(f32[16,256,256]{2,1,0:T(8,128)} %get-tuple-element.195, f32[256,256]{1,0:T(8,128)S(1)} %maximum_convert_fusion.3, f32[16]{0:T(128)S(1)} %get-tuple-element.186, f32[16]{0:T(128)S(1)} %get-tuple-element.187, pred[]{:T(512)S(6)} %compare.3), kind=kLoop, calls=%fused_computation.1.clone.1 | loop fusion | flops 4194304 | bytes 8650881 | tf_op jit(solution)/shard_map/while/body/eval_jaxpr/add | solution.py:31
  41.8 5.0 %select_add_fusion.2 = f32[16,256,256]{2,1,0:T(8,128)} fusion(f32[16,256,256]{2,1,0:T(8,128)} %get-tuple-element.195, f32[256,256]{1,0:T(8,128)S(1)} %maximum_convert_fusion.3, f32[16]{0:T(128)S(1)} %get-tuple-element.186, f32[16]{0:T(128)S(1)} %get-tuple-element.187, pred[]{:T(512)S(6)} %compare.3), kind=kLoop, calls=%fused_computation.1.clone.1 | loop fusion | flops 4194304 | bytes 8650881 | tf_op jit(solution)/shard_map/while/body/eval_jaxpr/add | solution.py:31
  46.9 5.0 %select_add_fusion.2 = f32[16,256,256]{2,1,0:T(8,128)} fusion(f32[16,256,256]{2,1,0:T(8,128)} %get-tuple-element.195, f32[256,256]{1,0:T(8,128)S(1)} %maximum_convert_fusion.3, f32[16]{0:T(128)S(1)} %get-tuple-element.186, f32[16]{0:T(128)S(1)} %get-tuple-element.187, pred[]{:T(512)S(6)} %compare.3), kind=kLoop, calls=%fused_computation.1.clone.1 | loop fusion | flops 4194304 | bytes 8650881 | tf_op jit(solution)/shard_map/while/body/eval_jaxpr/add | solution.py:31
  52.0 5.0 %select_add_fusion.2 = f32[16,256,256]{2,1,0:T(8,128)} fusion(f32[16,256,256]{2,1,0:T(8,128)} %get-tuple-element.195, f32[256,256]{1,0:T(8,128)S(1)} %maximum_convert_fusion.3, f32[16]{0:T(128)S(1)} %get-tuple-element.186, f32[16]{0:T(128)S(1)} %get-tuple-element.187, pred[]{:T(512)S(6)} %compare.3), kind=kLoop, calls=%fused_computation.1.clone.1 | loop fusion | flops 4194304 | bytes 8650881 | tf_op jit(solution)/shard_map/while/body/eval_jaxpr/add | solution.py:31
  57.0 5.0 %select_add_fusion.2 = f32[16,256,256]{2,1,0:T(8,128)} fusion(f32[16,256,256]{2,1,0:T(8,128)} %get-tuple-element.195, f32[256,256]{1,0:T(8,128)S(1)} %maximum_convert_fusion.3, f32[16]{0:T(128)S(1)} %get-tuple-element.186, f32[16]{0:T(128)S(1)} %get-tuple-element.187, pred[]{:T(512)S(6)} %compare.3), kind=kLoop, calls=%fused_computation.1.clone.1 | loop fusion | flops 4194304 | bytes 8650881 | tf_op jit(solution)/shard_map/while/body/eval_jaxpr/add | solution.py:31
  62.1 5.0 %select_add_fusion.2 = f32[16,256,256]{2,1,0:T(8,128)} fusion(f32[16,256,256]{2,1,0:T(8,128)} %get-tuple-element.195, f32[256,256]{1,0:T(8,128)S(1)} %maximum_convert_fusion.3, f32[16]{0:T(128)S(1)} %get-tuple-element.186, f32[16]{0:T(128)S(1)} %get-tuple-element.187, pred[]{:T(512)S(6)} %compare.3), kind=kLoop, calls=%fused_computation.1.clone.1 | loop fusion | flops 4194304 | bytes 8650881 | tf_op jit(solution)/shard_map/while/body/eval_jaxpr/add | solution.py:31
  67.2 5.0 %select_add_fusion.2 = f32[16,256,256]{2,1,0:T(8,128)} fusion(f32[16,256,256]{2,1,0:T(8,128)} %get-tuple-element.195, f32[256,256]{1,0:T(8,128)S(1)} %maximum_convert_fusion.3, f32[16]{0:T(128)S(1)} %get-tuple-element.186, f32[16]{0:T(128)S(1)} %get-tuple-element.187, pred[]{:T(512)S(6)} %compare.3), kind=kLoop, calls=%fused_computation.1.clone.1 | loop fusion | flops 4194304 | bytes 8650881 | tf_op jit(solution)/shard_map/while/body/eval_jaxpr/add | solution.py:31
  72.3 5.0 %select_add_fusion.2 = f32[16,256,256]{2,1,0:T(8,128)} fusion(f32[16,256,256]{2,1,0:T(8,128)} %get-tuple-element.195, f32[256,256]{1,0:T(8,128)S(1)} %maximum_convert_fusion.3, f32[16]{0:T(128)S(1)} %get-tuple-element.186, f32[16]{0:T(128)S(1)} %get-tuple-element.187, pred[]{:T(512)S(6)} %compare.3), kind=kLoop, calls=%fused_computation.1.clone.1 | loop fusion | flops 4194304 | bytes 8650881 | tf_op jit(solution)/shard_map/while/body/eval_jaxpr/add | solution.py:31
  77.4 5.0 %select_add_fusion.2 = f32[16,256,256]{2,1,0:T(8,128)} fusion(f32[16,256,256]{2,1,0:T(8,128)} %get-tuple-element.195, f32[256,256]{1,0:T(8,128)S(1)} %maximum_convert_fusion.3, f32[16]{0:T(128)S(1)} %get-tuple-element.186, f32[16]{0:T(128)S(1)} %get-tuple-element.187, pred[]{:T(512)S(6)} %compare.3), kind=kLoop, calls=%fused_computation.1.clone.1 | loop fusion | flops 4194304 | bytes 8650881 | tf_op jit(solution)/shard_map/while/body/eval_jaxpr/add | solution.py:31
  82.5 5.0 %select_add_fusion.2 = f32[16,256,256]{2,1,0:T(8,128)} fusion(f32[16,256,256]{2,1,0:T(8,128)} %get-tuple-element.195, f32[256,256]{1,0:T(8,128)S(1)} %maximum_convert_fusion.3, f32[16]{0:T(128)S(1)} %get-tuple-element.186, f32[16]{0:T(128)S(1)} %get-tuple-element.187, pred[]{:T(512)S(6)} %compare.3), kind=kLoop, calls=%fused_computation.1.clone.1 | loop fusion | flops 4194304 | bytes 8650881 | tf_op jit(solution)/shard_map/while/body/eval_jaxpr/add | solution.py:31
  87.5 5.0 %select_add_fusion.2 = f32[16,256,256]{2,1,0:T(8,128)} fusion(f32[16,256,256]{2,1,0:T(8,128)} %get-tuple-element.195, f32[256,256]{1,0:T(8,128)S(1)} %maximum_convert_fusion.3, f32[16]{0:T(128)S(1)} %get-tuple-element.186, f32[16]{0:T(128)S(1)} %get-tuple-element.187, pred[]{:T(512)S(6)} %compare.3), kind=kLoop, calls=%fused_computation.1.clone.1 | loop fusion | flops 4194304 | bytes 8650881 | tf_op jit(solution)/shard_map/while/body/eval_jaxpr/add | solution.py:31
  92.6 0.6 copy_bitcast_fusion
  93.2 0.6 copy_bitcast_fusion.2
  93.8 0.6 copy_bitcast_fusion.4
  94.4 0.7 copy.28
  95.2 0.7 copy.111
  95.9 0.9 maximum_convert_fusion.1
  96.8 7.0 %fusion.19 = f32[512,3,512]{0,2,1:T(8,128)S(1)} fusion(f32[518,3,512]{0,2,1:T(8,128)S(1)} %maximum_convert_fusion.1, f32[3,512]{1,0:T(4,128)S(1)} %copy-done.6, f32[3,512]{1,0:T(4,128)S(1)} %copy-done.7, f32[3,512]{1,0:T(4,128)S(1)} %copy-done.8, f32[3,512]{1,0:T(4,128)S(1)} %copy-done.9, f32[3,512]{1,0:T(4,128)S(1)} %copy-done.10, ...), kind=kLoop, calls=%fused_computation.24 | loop fusion | flops 10223616 | bytes 25208832 | tf_op jit(solution)/shard_map/add | solution.py:71
  103.9 0.9 fusion.55
  104.8 10.8 %all-to-all-start = ((bf16[32,16,512]{2,1,0:T(8,128)(2,1)}), bf16[32,16,512]{2,1,0:T(8,128)(2,1)}, u32[]{:S(2)}, u32[]{:S(2)}) async-start(bf16[32,16,512]{2,1,0:T(8,128)(2,1)} %bitcast.103), calls=%async_computation | async-start | bytes 1048576 | tf_op jit(solution)/shard_map/all_to_all | solution.py:76
  116.0 0.8 dynamic_slice.26
  117.0 13.6 %all-to-all-done = bf16[32,16,512]{2,1,0:T(8,128)(2,1)} async-done(((bf16[32,16,512]{2,1,0:T(8,128)(2,1)}), bf16[32,16,512]{2,1,0:T(8,128)(2,1)}, u32[]{:S(2)}, u32[]{:S(2)}) %all-to-all-start) | async-done | bytes 524320 | tf_op jit(solution)/shard_map/all_to_all | solution.py:76
  130.5 2.1 copy.29
  132.7 2.0 reshape.174
  134.7 1.6 fusion.85
  136.3 14.1 %fusion.5 = f32[16,16,1,64]{3,2,1,0:T(1,128)S(1)} fusion(f32[16,16,64,1]{2,3,1,0:T(1,128)S(1)} %bitcast.108, f32[64,64]{1,0:T(8,128)S(1)} %multiply_convert_fusion, f32[16,16]{1,0:T(8,128)S(1)} %copy.30, pred[64,64]{1,0:T(8,128)(4,1)S(1)} %fusion.97), kind=kOutput, calls=%fused_computation.10 | convolution fusion | flops 14680064 | bytes 152576 | tf_op jit(solution)/shard_map/cnkb,cnb->cnk/dot_general | solution.py:54
  150.5 1.2 fusion.82
  151.7 3.3 fusion.45
  155.0 2.0 convert_element_type.86
  157.0 1.3 copy.33
  158.4 21.9 %all_to_all.26 = bf16[16,32,512]{2,0,1:T(8,128)(2,1)S(1)} all-to-all(bf16[16,32,512]{2,0,1:T(8,128)(2,1)S(1)} %copy.33), channel_id=1, replica_groups=mesh['ctx'=32,'tp'=8] {'ctx'}, dimensions={1} | all-to-all | bytes 1048576 | tf_op jit(solution)/shard_map/all_to_all | solution.py:84
  180.3 1.0 fusion.57
  181.3 0.8 copy.34
  182.3 2.0 copy.47
  184.3 89.4 %all-gather.3.cloned.1.call-done = bf16[512,4096]{0,1:T(8,128)(2,1)} async-done(((bf16[512,512]{0,1:T(8,128)(2,1)}), bf16[512,4096]{0,1:T(8,128)(2,1)}) %all-gather.3.cloned.1.call-update) | async-done | bytes 4194320 | tf_op jit(solution)/shard_map/all_gather | solution.py:86
  273.8 3.1 fusion.2
  276.9 71.4 %all-gather.5.cloned.1.call-done = bf16[4096,3,256]{0,2,1:T(8,128)(2,1)} async-done(((bf16[128,3,256]{0,2,1:T(8,128)(2,1)}), bf16[4096,3,256]{0,2,1:T(8,128)(2,1)}) %all-gather.5.cloned.1.call-update) | async-done | bytes 6291472 | tf_op jit(solution)/shard_map/all_gather | solution.py:91
  348.3 8.2 %fusion.36 = bf16[512,768]{1,0:T(8,128)(2,1)S(1)} fusion(bf16[4096,768]{0,1:T(8,128)(2,1)} %bitcast.112, bf16[512,4096]{0,1:T(8,128)(2,1)} %all-gather.3.cloned.1.call-done, f32[4096]{0:T(1024)S(1)} %copy-done.12, f32[512]{0:T(512)S(1)} %add_rsqrt_fusion), kind=kOutput, calls=%fused_computation.54 | convolution fusion | flops 3230007296 | bytes 11290624 | tf_op jit(solution)/shard_map/dot_general | solution.py:93
  356.5 2.2 collective-permute-start.1
  358.8 0.8 copy.54
  359.7 1.9 fusion.27
  361.5 11.9 %collective-permute-done.1 = bf16[512,512]{1,0:T(8,128)(2,1)} collective-permute-done((bf16[512,512]{1,0:T(8,128)(2,1)S(1)}, bf16[512,512]{1,0:T(8,128)(2,1)}, u32[]{:S(2)}, u32[]{:S(2)}) %collective-permute-start.1) | collective-permute-done | bytes 524320 | tf_op jit(solution)/shard_map/ppermute | solution.py:18
  373.4 2.2 collective-permute-start.2
  375.6 1.1 fusion.107
  376.8 0.4 fusion.28
  377.3 16.9 %collective-permute-done.2 = bf16[512,512]{1,0:T(8,128)(2,1)} collective-permute-done((bf16[512,512]{1,0:T(8,128)(2,1)}, bf16[512,512]{1,0:T(8,128)(2,1)}, u32[]{:S(2)}, u32[]{:S(2)}) %collective-permute-start.2) | collective-permute-done | bytes 524320 | tf_op jit(solution)/shard_map/ppermute | solution.py:18
  394.2 1.1 fusion.106
  395.2 0.9 copy.56
  396.6 2.5 fusion.53
  399.1 1.3 fusion.32
  400.5 0.6 convolution_add_fusion.1
  401.4 0.6 fusion.50
  402.0 0.8 copy.48
  (81 shorter events, 2.5 us)
Async XLA Ops:
  8.9 87.0 %collective-permute-start = (bf16[6,3,512]{0,2,1:T(8,128)(2,1)}, bf16[6,3,512]{0,2,1:T(8,128)(2,1)S(1)}, u32[]{:S(2)}, u32[]{:S(2)}) collective-permute-start(bf16[6,3,512]{0,2,1:T(8,128)(2,1)} %copy.27), channel_id=1, source_target_pairs={{0,8},{8,16},{16,24},{24,32},{32,40},{40,48},{48,56},{56,64},{64,7... | collective-permute-start | bytes 55304 | tf_op jit(solution)/shard_map/ppermute | solution.py:18
  13.4 81.0 %copy-start.3 = (bf16[512,3,512]{2,0,1:T(8,128)(2,1)S(1)}, bf16[512,3,512]{2,0,1:T(8,128)(2,1)}, u32[]{:S(2)}) copy-start(bf16[512,3,512]{2,0,1:T(8,128)(2,1)} %param.9) | copy-start | bytes 4718596
  95.1 1.7 copy-start.6
  95.1 1.7 copy-start.7
  95.1 1.7 copy-start.8
  95.1 1.7 copy-start.9
  95.2 1.7 copy-start.10
  95.2 1.7 copy-start.11
  104.8 25.7 %all-to-all-start = ((bf16[32,16,512]{2,1,0:T(8,128)(2,1)}), bf16[32,16,512]{2,1,0:T(8,128)(2,1)}, u32[]{:S(2)}, u32[]{:S(2)}) async-start(bf16[32,16,512]{2,1,0:T(8,128)(2,1)} %bitcast.103), calls=%async_computation | async-start | bytes 1048576 | tf_op jit(solution)/shard_map/all_to_all | solution.py:76
  115.6 158.1 %all-gather.3.cloned.1.call-start = ((), (), s32[]{:S(2)}) async-start(), calls=%async_computation.2 | async-start | bytes 4718592 | tf_op jit(solution)/shard_map/all_gather | solution.py:86
  136.3 15.4 %copy-start = (f32[16,256,256]{2,1,0:T(8,128)S(1)}, f32[16,256,256]{2,1,0:T(8,128)}, u32[]{:S(2)}) copy-start(f32[16,256,256]{2,1,0:T(8,128)} %get-tuple-element.96) | copy-start | bytes 12582916
  136.3 15.4 %copy-start.1 = (bf16[16,64,256]{2,1,0:T(8,128)(2,1)S(1)}, bf16[16,64,256]{2,1,0:T(8,128)(2,1)}, u32[]{:S(2)}) copy-start(bf16[16,64,256]{2,1,0:T(8,128)(2,1)} %reshape.174) | copy-start | bytes 1572868
  155.0 26.3 %copy-start.5 = (bf16[128,3,256]{2,0,1:T(8,128)(2,1)S(1)}, bf16[128,3,256]{2,0,1:T(8,128)(2,1)}, u32[]{:S(2)}) copy-start(bf16[128,3,256]{2,0,1:T(8,128)(2,1)} %param.15) | copy-start | bytes 589828
  181.3 167.0 %copy-start.12 = (f32[4096]{0:T(1024)S(1)}, f32[4096]{0:T(1024)}, u32[]{:S(2)}) copy-start(f32[4096]{0:T(1024)} %param.14) | copy-start | bytes 49156
  181.3 167.0 %all-gather.5.cloned.1.call-start = ((), (), s32[]{:S(2)}) async-start(), calls=%async_computation.3 | async-start | bytes 6488064 | tf_op jit(solution)/shard_map/all_gather | solution.py:91
  356.5 16.9 %collective-permute-start.1 = (bf16[512,512]{1,0:T(8,128)(2,1)S(1)}, bf16[512,512]{1,0:T(8,128)(2,1)}, u32[]{:S(2)}, u32[]{:S(2)}) collective-permute-start(bf16[512,512]{1,0:T(8,128)(2,1)S(1)} %slice.119), channel_id=1, source_target_pairs={{0,8},{8,16},{16,24},{24,32},{32,40},{40,48},{48,56},{56,64},{64,7... | collective-permute-start | bytes 1572872 | tf_op jit(solution)/shard_map/ppermute | solution.py:18
  373.4 20.7 %collective-permute-start.2 = (bf16[512,512]{1,0:T(8,128)(2,1)}, bf16[512,512]{1,0:T(8,128)(2,1)}, u32[]{:S(2)}, u32[]{:S(2)}) collective-permute-start(bf16[512,512]{1,0:T(8,128)(2,1)} %collective-permute-done.1), channel_id=1, source_target_pairs={{0,8},{8,16},{16,24},{24,32},{32,40},{40,48},{48,56},{56,64},{64,7... | collective-permute-start | bytes 1572872 | tf_op jit(solution)/shard_map/ppermute | solution.py:18
  396.1 3.0 copy-start.2
  400.4 1.0 copy-start.4
Sparse Core Ops, SparseCore 0:
  181.4 92.3 all-gather.2
  276.8 71.4 all-gather.4
where the time goes:
time: 411 us; the launch traced here: 410 us
  waiting for transfers between devices  203 us (49%)
  other arithmetic  94.5 us (23%)
  matrix products  34.9 us (8%)
  local copies, waits for them, and re-layouts  23.4 us (6%)
  blocking collectives  21.9 us (5%)
  starting transfers between devices  17.3 us (4%)
  between operations  14.4 us (4%)
    all_gather x1, waiting for transfers between devices, on_device(): gathered = lax.all_gather(mixer, 'tp', axis=1, tiled=True)  89.4 us
    add x16, other arithmetic, add_mode(): return running + term  78.5 us
    all_gather x1, waiting for transfers between devices, on_device(): shard_rows = lax.all_gather(qkv_weight, 'ctx', axis=0, tiled=True)  71.4 us
    ppermute x3, waiting for transfers between devices, from_behind(): lax.ppermute(value, axis, [(source, source + steps) for source in range(l...  28.8 us
    all_to_all x1, blocking collectives, on_device(): lax.all_to_all(filtered, 'ctx', split_axis=1, concat_axis=0, tiled=True)  21.9 us
    dot_general x1, matrix products, channel_conv(): entering = jnp.einsum('cnkb,cnb->cnk', carry, block_ends, precision=PRECISE)  14.1 us
    all_to_all x1, waiting for transfers between devices, on_device(): lax.all_to_all(gated.T, 'ctx', split_axis=0, concat_axis=1, tiled=True)  13.6 us
    all_to_all x1, starting transfers between devices, on_device(): lax.all_to_all(gated.T, 'ctx', split_axis=0, concat_axis=1, tiled=True)  10.8 us
  transfers between devices with their start and end apart: 6, of which 5 were waited for; matrix products, arithmetic and copies ran while one was open for 24% of the time, Pallas kernels for 0%

commit v1 on v0

--- a/solution.py
+++ b/solution.py
@@ -83,7 +83,9 @@
     ).astype(jnp.bfloat16)
     long_part = lax.all_to_all(filtered, "ctx", split_axis=1, concat_axis=0, tiled=True).T
     mixer = (short_conv[:, 0] * long_part.astype(jnp.float32)).astype(jnp.bfloat16)
-    gathered = lax.all_gather(mixer, "tp", axis=1, tiled=True)
+    gathered = jnp.concatenate(
+        lax.all_to_all(jnp.stack([mixer] * lax.axis_size("tp")), "tp", 0, 0), axis=1
+    )
     as_float = gathered.astype(jnp.float32)
     inverse = lax.rsqrt(jnp.mean(as_float * as_float, axis=1, keepdims=True) + EPSILON)
     normed = (as_float * inverse * norm_gain[None]).astype(jnp.bfloat16)

time: 411 us -> 310 us (0.75)
  waiting for transfers between devices: 203 us -> 89.8 us
  starting transfers between devices: 17.3 us -> 22.8 us
  other arithmetic: 94.5 us -> 99.4 us
    all_gather x1 -> x0, waiting for transfers between devices: 89.4 us -> none  [on_device(): gathered = lax.all_gather(mixer, 'tp', axis=1, tiled=True)]
    all_gather x1, waiting for transfers between devices: 71.4 us -> 0.01 us  [on_device(): shard_rows = lax.all_gather(qkv_weight, 'ctx', axis=0, tiled=True)]
    all_to_all x0 -> x1, waiting for transfers between devices: none -> 48.8 us  [on_device(): lax.all_to_all(jnp.stack([mixer] * lax.axis_size('tp')), 'tp', 0, 0)]
    all_to_all x0 -> x1, starting transfers between devices: none -> 5.81 us  [on_device(): lax.all_to_all(jnp.stack([mixer] * lax.axis_size('tp')), 'tp', 0, 0)]
    convert_element_type x0 -> x1, other arithmetic: none -> 4.18 us  [on_device(): normed = (as_float * inverse * norm_gain[None]).astype(jnp.bfloat16)]
  transfers between devices with their start and end apart: 6 -> 6, of which waited for: 5 -> 4; matrix products, arithmetic and copies ran while one was open for 24% -> 46% of each run, Pallas kernels for 0% -> 0%
where the time goes in v1:
time: 310 us; the launch traced here: 309 us
  other arithmetic  99.4 us (32%)
  waiting for transfers between devices  89.8 us (29%)
  matrix products  34.3 us (11%)
  local copies, waits for them, and re-layouts  26.4 us (9%)
  starting transfers between devices  22.8 us (7%)
  blocking collectives  21.4 us (7%)
  between operations  14.4 us (5%)
    add x16, other arithmetic, add_mode(): return running + term  80 us
    all_to_all x1, waiting for transfers between devices, on_device(): lax.all_to_all(jnp.stack([mixer] * lax.axis_size('tp')), 'tp', 0, 0)  48.8 us
    ppermute x3, waiting for transfers between devices, from_behind(): lax.ppermute(value, axis, [(source, source + steps) for source in range(l...  27.6 us
    all_to_all x1, blocking collectives, on_device(): lax.all_to_all(filtered, 'ctx', split_axis=1, concat_axis=0, tiled=True)  21.4 us
    dot_general x1, matrix products, channel_conv(): entering = jnp.einsum('cnkb,cnb->cnk', carry, block_ends, precision=PRECISE)  14.1 us
    all_to_all x1, waiting for transfers between devices, on_device(): lax.all_to_all(gated.T, 'ctx', split_axis=0, concat_axis=1, tiled=True)  13.4 us
    all_to_all x1, starting transfers between devices, on_device(): lax.all_to_all(gated.T, 'ctx', split_axis=0, concat_axis=1, tiled=True)  11 us
    unnamed x37, local copies, waits for them, and re-layouts  8.11 us
  transfers between devices with their start and end apart: 6, of which 4 were waited for; matrix products, arithmetic and copies ran while one was open for 46% of the time, Pallas kernels for 0%

profile of v1, /device:TPU:128, one launch (start us, length us, event | category | flops | bytes accessed | tf_op | source)
XLA Modules:
  0.0 308.6 jit_solution(7849500866267992889)
XLA Ops:
  7.2 0.7 slice.81
  8.0 1.0 copy.27
  8.9 1.9 collective-permute-start
  10.8 1.7 copy.34
  12.6 1.8 fusion.101
  14.4 0.8 sqrt_multiply_fusion
  15.2 80.7 %while.14 = (s32[]{:T(128)}, f32[16,256,256]{2,1,0:T(8,128)}, f32[16,16]{1,0:T(8,128)S(1)}, f32[16,16]{1,0:T(8,128)S(1)}, s32[]{:T(128)}, /*index=5*/s32[]{:T(128)}) while((s32[]{:T(128)}, f32[16,256,256]{2,1,0:T(8,128)}, f32[16,16]{1,0:T(8,128)S(1)}, f32[16,16]{1,0:T(8,128)S(1)}, s32[]{:T(128)}, /*index=5*/s32[]{:T(128)}) %tuple.60), condition=%wide.region_1.2_spmd.clone, body=%wide.region_0.1_spmd.clone.sunk | while | flops 4390931 | bytes 8913363 | solution.py:33
  15.3 2.9 select_add_fusion.2
  18.3 5.1 %select_add_fusion.2 = f32[16,256,256]{2,1,0:T(8,128)} fusion(f32[16,256,256]{2,1,0:T(8,128)} %get-tuple-element.195, f32[256,256]{1,0:T(8,128)S(1)} %maximum_convert_fusion.3, f32[16]{0:T(128)S(1)} %get-tuple-element.186, f32[16]{0:T(128)S(1)} %get-tuple-element.187, pred[]{:T(512)S(6)} %compare.3), kind=kLoop, calls=%fused_computation.1.clone.1 | loop fusion | flops 4194304 | bytes 8650881 | tf_op jit(solution)/shard_map/while/body/eval_jaxpr/add | solution.py:31
  23.4 5.1 %select_add_fusion.2 = f32[16,256,256]{2,1,0:T(8,128)} fusion(f32[16,256,256]{2,1,0:T(8,128)} %get-tuple-element.195, f32[256,256]{1,0:T(8,128)S(1)} %maximum_convert_fusion.3, f32[16]{0:T(128)S(1)} %get-tuple-element.186, f32[16]{0:T(128)S(1)} %get-tuple-element.187, pred[]{:T(512)S(6)} %compare.3), kind=kLoop, calls=%fused_computation.1.clone.1 | loop fusion | flops 4194304 | bytes 8650881 | tf_op jit(solution)/shard_map/while/body/eval_jaxpr/add | solution.py:31
  28.6 5.1 %select_add_fusion.2 = f32[16,256,256]{2,1,0:T(8,128)} fusion(f32[16,256,256]{2,1,0:T(8,128)} %get-tuple-element.195, f32[256,256]{1,0:T(8,128)S(1)} %maximum_convert_fusion.3, f32[16]{0:T(128)S(1)} %get-tuple-element.186, f32[16]{0:T(128)S(1)} %get-tuple-element.187, pred[]{:T(512)S(6)} %compare.3), kind=kLoop, calls=%fused_computation.1.clone.1 | loop fusion | flops 4194304 | bytes 8650881 | tf_op jit(solution)/shard_map/while/body/eval_jaxpr/add | solution.py:31
  33.7 5.1 %select_add_fusion.2 = f32[16,256,256]{2,1,0:T(8,128)} fusion(f32[16,256,256]{2,1,0:T(8,128)} %get-tuple-element.195, f32[256,256]{1,0:T(8,128)S(1)} %maximum_convert_fusion.3, f32[16]{0:T(128)S(1)} %get-tuple-element.186, f32[16]{0:T(128)S(1)} %get-tuple-element.187, pred[]{:T(512)S(6)} %compare.3), kind=kLoop, calls=%fused_computation.1.clone.1 | loop fusion | flops 4194304 | bytes 8650881 | tf_op jit(solution)/shard_map/while/body/eval_jaxpr/add | solution.py:31
  38.9 5.1 %select_add_fusion.2 = f32[16,256,256]{2,1,0:T(8,128)} fusion(f32[16,256,256]{2,1,0:T(8,128)} %get-tuple-element.195, f32[256,256]{1,0:T(8,128)S(1)} %maximum_convert_fusion.3, f32[16]{0:T(128)S(1)} %get-tuple-element.186, f32[16]{0:T(128)S(1)} %get-tuple-element.187, pred[]{:T(512)S(6)} %compare.3), kind=kLoop, calls=%fused_computation.1.clone.1 | loop fusion | flops 4194304 | bytes 8650881 | tf_op jit(solution)/shard_map/while/body/eval_jaxpr/add | solution.py:31
  44.0 5.1 %select_add_fusion.2 = f32[16,256,256]{2,1,0:T(8,128)} fusion(f32[16,256,256]{2,1,0:T(8,128)} %get-tuple-element.195, f32[256,256]{1,0:T(8,128)S(1)} %maximum_convert_fusion.3, f32[16]{0:T(128)S(1)} %get-tuple-element.186, f32[16]{0:T(128)S(1)} %get-tuple-element.187, pred[]{:T(512)S(6)} %compare.3), kind=kLoop, calls=%fused_computation.1.clone.1 | loop fusion | flops 4194304 | bytes 8650881 | tf_op jit(solution)/shard_map/while/body/eval_jaxpr/add | solution.py:31
  49.2 5.1 %select_add_fusion.2 = f32[16,256,256]{2,1,0:T(8,128)} fusion(f32[16,256,256]{2,1,0:T(8,128)} %get-tuple-element.195, f32[256,256]{1,0:T(8,128)S(1)} %maximum_convert_fusion.3, f32[16]{0:T(128)S(1)} %get-tuple-element.186, f32[16]{0:T(128)S(1)} %get-tuple-element.187, pred[]{:T(512)S(6)} %compare.3), kind=kLoop, calls=%fused_computation.1.clone.1 | loop fusion | flops 4194304 | bytes 8650881 | tf_op jit(solution)/shard_map/while/body/eval_jaxpr/add | solution.py:31
  54.4 5.2 %select_add_fusion.2 = f32[16,256,256]{2,1,0:T(8,128)} fusion(f32[16,256,256]{2,1,0:T(8,128)} %get-tuple-element.195, f32[256,256]{1,0:T(8,128)S(1)} %maximum_convert_fusion.3, f32[16]{0:T(128)S(1)} %get-tuple-element.186, f32[16]{0:T(128)S(1)} %get-tuple-element.187, pred[]{:T(512)S(6)} %compare.3), kind=kLoop, calls=%fused_computation.1.clone.1 | loop fusion | flops 4194304 | bytes 8650881 | tf_op jit(solution)/shard_map/while/body/eval_jaxpr/add | solution.py:31
  59.6 5.1 %select_add_fusion.2 = f32[16,256,256]{2,1,0:T(8,128)} fusion(f32[16,256,256]{2,1,0:T(8,128)} %get-tuple-element.195, f32[256,256]{1,0:T(8,128)S(1)} %maximum_convert_fusion.3, f32[16]{0:T(128)S(1)} %get-tuple-element.186, f32[16]{0:T(128)S(1)} %get-tuple-element.187, pred[]{:T(512)S(6)} %compare.3), kind=kLoop, calls=%fused_computation.1.clone.1 | loop fusion | flops 4194304 | bytes 8650881 | tf_op jit(solution)/shard_map/while/body/eval_jaxpr/add | solution.py:31
  64.8 5.2 %select_add_fusion.2 = f32[16,256,256]{2,1,0:T(8,128)} fusion(f32[16,256,256]{2,1,0:T(8,128)} %get-tuple-element.195, f32[256,256]{1,0:T(8,128)S(1)} %maximum_convert_fusion.3, f32[16]{0:T(128)S(1)} %get-tuple-element.186, f32[16]{0:T(128)S(1)} %get-tuple-element.187, pred[]{:T(512)S(6)} %compare.3), kind=kLoop, calls=%fused_computation.1.clone.1 | loop fusion | flops 4194304 | bytes 8650881 | tf_op jit(solution)/shard_map/while/body/eval_jaxpr/add | solution.py:31
  70.1 5.1 %select_add_fusion.2 = f32[16,256,256]{2,1,0:T(8,128)} fusion(f32[16,256,256]{2,1,0:T(8,128)} %get-tuple-element.195, f32[256,256]{1,0:T(8,128)S(1)} %maximum_convert_fusion.3, f32[16]{0:T(128)S(1)} %get-tuple-element.186, f32[16]{0:T(128)S(1)} %get-tuple-element.187, pred[]{:T(512)S(6)} %compare.3), kind=kLoop, calls=%fused_computation.1.clone.1 | loop fusion | flops 4194304 | bytes 8650881 | tf_op jit(solution)/shard_map/while/body/eval_jaxpr/add | solution.py:31
  75.2 5.2 %select_add_fusion.2 = f32[16,256,256]{2,1,0:T(8,128)} fusion(f32[16,256,256]{2,1,0:T(8,128)} %get-tuple-element.195, f32[256,256]{1,0:T(8,128)S(1)} %maximum_convert_fusion.3, f32[16]{0:T(128)S(1)} %get-tuple-element.186, f32[16]{0:T(128)S(1)} %get-tuple-element.187, pred[]{:T(512)S(6)} %compare.3), kind=kLoop, calls=%fused_computation.1.clone.1 | loop fusion | flops 4194304 | bytes 8650881 | tf_op jit(solution)/shard_map/while/body/eval_jaxpr/add | solution.py:31
  80.5 5.1 %select_add_fusion.2 = f32[16,256,256]{2,1,0:T(8,128)} fusion(f32[16,256,256]{2,1,0:T(8,128)} %get-tuple-element.195, f32[256,256]{1,0:T(8,128)S(1)} %maximum_convert_fusion.3, f32[16]{0:T(128)S(1)} %get-tuple-element.186, f32[16]{0:T(128)S(1)} %get-tuple-element.187, pred[]{:T(512)S(6)} %compare.3), kind=kLoop, calls=%fused_computation.1.clone.1 | loop fusion | flops 4194304 | bytes 8650881 | tf_op jit(solution)/shard_map/while/body/eval_jaxpr/add | solution.py:31
  85.7 5.1 %select_add_fusion.2 = f32[16,256,256]{2,1,0:T(8,128)} fusion(f32[16,256,256]{2,1,0:T(8,128)} %get-tuple-element.195, f32[256,256]{1,0:T(8,128)S(1)} %maximum_convert_fusion.3, f32[16]{0:T(128)S(1)} %get-tuple-element.186, f32[16]{0:T(128)S(1)} %get-tuple-element.187, pred[]{:T(512)S(6)} %compare.3), kind=kLoop, calls=%fused_computation.1.clone.1 | loop fusion | flops 4194304 | bytes 8650881 | tf_op jit(solution)/shard_map/while/body/eval_jaxpr/add | solution.py:31
  90.8 5.1 %select_add_fusion.2 = f32[16,256,256]{2,1,0:T(8,128)} fusion(f32[16,256,256]{2,1,0:T(8,128)} %get-tuple-element.195, f32[256,256]{1,0:T(8,128)S(1)} %maximum_convert_fusion.3, f32[16]{0:T(128)S(1)} %get-tuple-element.186, f32[16]{0:T(128)S(1)} %get-tuple-element.187, pred[]{:T(512)S(6)} %compare.3), kind=kLoop, calls=%fused_computation.1.clone.1 | loop fusion | flops 4194304 | bytes 8650881 | tf_op jit(solution)/shard_map/while/body/eval_jaxpr/add | solution.py:31
  95.9 0.6 copy_bitcast_fusion
  96.5 0.6 copy_bitcast_fusion.2
  97.1 0.6 copy_bitcast_fusion.4
  97.8 0.7 copy.28
  98.5 0.7 copy.111
  99.3 0.9 maximum_convert_fusion.1
  100.2 7.0 %fusion.15 = f32[512,3,512]{0,2,1:T(8,128)S(1)} fusion(f32[518,3,512]{0,2,1:T(8,128)S(1)} %maximum_convert_fusion.1, f32[3,512]{1,0:T(4,128)S(1)} %copy-done.7, f32[3,512]{1,0:T(4,128)S(1)} %copy-done.8, f32[3,512]{1,0:T(4,128)S(1)} %copy-done.9, f32[3,512]{1,0:T(4,128)S(1)} %copy-done.10, f32[3,512]{1,0:T(4,128)S(1)} %copy-done.11, ...), kind=kLoop, calls=%fused_computation.21 | loop fusion | flops 10223616 | bytes 25208832 | tf_op jit(solution)/shard_map/add | solution.py:71
  107.2 0.9 fusion.48
  108.2 11.0 %all-to-all-start = ((bf16[32,16,512]{2,1,0:T(8,128)(2,1)}), bf16[32,16,512]{2,1,0:T(8,128)(2,1)}, u32[]{:S(2)}, u32[]{:S(2)}) async-start(bf16[32,16,512]{2,1,0:T(8,128)(2,1)} %bitcast.108), calls=%async_computation | async-start | bytes 1048576 | tf_op jit(solution)/shard_map/all_to_all | solution.py:76
  119.3 0.8 dynamic_slice.26
  120.3 13.4 %all-to-all-done = bf16[32,16,512]{2,1,0:T(8,128)(2,1)} async-done(((bf16[32,16,512]{2,1,0:T(8,128)(2,1)}), bf16[32,16,512]{2,1,0:T(8,128)(2,1)}, u32[]{:S(2)}, u32[]{:S(2)}) %all-to-all-start) | async-done | bytes 524320 | tf_op jit(solution)/shard_map/all_to_all | solution.py:76
  133.7 2.1 copy.29
  135.8 2.0 reshape.189
  137.8 1.6 fusion.78
  139.5 14.1 %fusion.5 = f32[16,16,1,64]{3,2,1,0:T(1,128)S(1)} fusion(f32[16,16,64,1]{2,3,1,0:T(1,128)S(1)} %bitcast.113, f32[64,64]{1,0:T(8,128)S(1)} %multiply_convert_fusion, f32[16,16]{1,0:T(8,128)S(1)} %copy.30, pred[64,64]{1,0:T(8,128)(4,1)S(1)} %fusion.90), kind=kOutput, calls=%fused_computation.10 | convolution fusion | flops 14680064 | bytes 152576 | tf_op jit(solution)/shard_map/cnkb,cnb->cnk/dot_general | solution.py:54
  153.6 1.2 fusion.75
  154.8 3.3 %fusion.38 = bf16[16,64,256]{2,1,0:T(8,128)(2,1)} fusion(f32[16,64,256]{2,1,0:T(8,128)S(1)} %fusion.75, bf16[16,64,256]{2,1,0:T(8,128)(2,1)S(1)} %copy-done.1, f32[16,256,256]{2,1,0:T(8,128)S(1)} %copy-done, pred[256,256]{1,0:T(8,128)(4,1)S(1)} %subtract_compare_fusion, f32[16]{0:T(128)S(1)} %dynamic_slice.26), kind=kOutput, calls=%fused_computation.54 | convolution fusion | flops 807665664 | bytes 6357056 | tf_op jit(solution)/shard_map/cts,cbs->cbt/dot_general | solution.py:58
  158.1 2.0 convert_element_type.95
  160.1 1.3 copy.33
  161.5 21.4 %all_to_all.31 = bf16[16,32,512]{2,0,1:T(8,128)(2,1)S(1)} all-to-all(bf16[16,32,512]{2,0,1:T(8,128)(2,1)S(1)} %copy.33), channel_id=1, replica_groups=mesh['ctx'=32,'tp'=8] {'ctx'}, dimensions={1} | all-to-all | bytes 1048576 | tf_op jit(solution)/shard_map/all_to_all | solution.py:84
  183.0 0.8 copy-done.2
  183.8 2.4 stack.2
  186.2 5.8 %all-to-all-start.2 = ((bf16[8,512,512]{1,2,0:T(8,128)(2,1)}), bf16[8,512,512]{1,2,0:T(8,128)(2,1)}, u32[]{:S(2)}, u32[]{:S(2)}) async-start(bf16[8,512,512]{1,2,0:T(8,128)(2,1)} %stack.2), calls=%async_computation.2 | async-start | bytes 8388608 | tf_op jit(solution)/shard_map/all_to_all | solution.py:87
  192.2 1.0 copy.47
  193.2 48.8 %all-to-all-done.2 = bf16[8,512,512]{1,2,0:T(8,128)(2,1)} async-done(((bf16[8,512,512]{1,2,0:T(8,128)(2,1)}), bf16[8,512,512]{1,2,0:T(8,128)(2,1)}, u32[]{:S(2)}, u32[]{:S(2)}) %all-to-all-start.2) | async-done | bytes 4194336 | tf_op jit(solution)/shard_map/all_to_all | solution.py:87
  242.0 3.1 %fusion.2 = f32[512]{0:T(512)S(1)} fusion(bf16[8,512,512]{1,2,0:T(8,128)(2,1)} %all-to-all-done.2), kind=kLoop, calls=%fused_computation.7 | loop fusion | flops 6290944 | bytes 4196352 | tf_op jit(solution)/shard_map/reduce_sum | solution.py:90
  245.1 4.2 %fusion.4 = bf16[8,512,512]{1,2,0:T(8,128)(2,1)} fusion(bf16[8,512,512]{1,2,0:T(8,128)(2,1)} %all-to-all-done.2, f32[8,512]{1,0:T(8,128)S(1)} %mul.274, f32[512]{0:T(512)S(1)} %add_rsqrt_fusion), kind=kLoop, calls=%fused_computation.9 | loop fusion | flops 8388608 | bytes 8407040 | tf_op jit(solution)/shard_map/convert_element_type | solution.py:91
  249.3 7.5 %convolution_convert_fusion = bf16[512,768]{1,0:T(8,128)(2,1)S(1)} fusion(bf16[512,4096]{0,1:T(8,128)(2,1)} %bitcast.107, bf16[4096,768]{0,1:T(8,128)(2,1)} %bitcast.117), kind=kOutput, calls=%fused_computation.51 | convolution fusion | flops 3221618688 | bytes 11272192 | tf_op jit(solution)/shard_map/dot_general | solution.py:95
  256.9 1.9 collective-permute-start.1
  258.9 0.8 copy.54
  259.7 1.9 fusion.23
  261.6 10.8 %collective-permute-done.1 = bf16[512,512]{1,0:T(8,128)(2,1)} collective-permute-done((bf16[512,512]{1,0:T(8,128)(2,1)S(1)}, bf16[512,512]{1,0:T(8,128)(2,1)}, u32[]{:S(2)}, u32[]{:S(2)}) %collective-permute-start.1) | collective-permute-done | bytes 524320 | tf_op jit(solution)/shard_map/ppermute | solution.py:18
  272.4 2.2 collective-permute-start.2
  274.6 1.1 fusion.100
  276.3 16.8 %collective-permute-done.2 = bf16[512,512]{1,0:T(8,128)(2,1)} collective-permute-done((bf16[512,512]{1,0:T(8,128)(2,1)}, bf16[512,512]{1,0:T(8,128)(2,1)}, u32[]{:S(2)}, u32[]{:S(2)}) %collective-permute-start.2) | collective-permute-done | bytes 524320 | tf_op jit(solution)/shard_map/ppermute | solution.py:18
  293.1 1.1 fusion.99
  294.2 0.9 copy.56
  295.5 2.5 fusion.46
  298.0 1.3 fusion.28
  300.3 0.6 fusion.43
  300.9 0.8 copy.48
  (85 shorter events, 3.4 us)
Async XLA Ops:
  7.2 242.1 %all-gather.2.cloned.1.call-start = ((), (), s32[]{:S(2)}) async-start(), calls=%async_computation.3 | async-start | bytes 6488064 | tf_op jit(solution)/shard_map/all_gather | solution.py:93
  8.9 90.3 %collective-permute-start = (bf16[6,3,512]{0,2,1:T(8,128)(2,1)}, bf16[6,3,512]{0,2,1:T(8,128)(2,1)S(1)}, u32[]{:S(2)}, u32[]{:S(2)}) collective-permute-start(bf16[6,3,512]{0,2,1:T(8,128)(2,1)} %copy.27), channel_id=1, source_target_pairs={{0,8},{8,16},{16,24},{24,32},{32,40},{40,48},{48,56},{56,64},{64,7... | collective-permute-start | bytes 55304 | tf_op jit(solution)/shard_map/ppermute | solution.py:18
  15.2 82.6 %copy-start.5 = (bf16[512,3,512]{2,0,1:T(8,128)(2,1)S(1)}, bf16[512,3,512]{2,0,1:T(8,128)(2,1)}, u32[]{:S(2)}) copy-start(bf16[512,3,512]{2,0,1:T(8,128)(2,1)} %param.9) | copy-start | bytes 4718596
  98.5 1.7 copy-start.7
  98.5 1.7 copy-start.8
  98.5 1.7 copy-start.9
  98.5 1.7 copy-start.10
  98.5 1.7 copy-start.11
  98.5 1.7 copy-start.12
  108.2 25.5 %all-to-all-start = ((bf16[32,16,512]{2,1,0:T(8,128)(2,1)}), bf16[32,16,512]{2,1,0:T(8,128)(2,1)}, u32[]{:S(2)}, u32[]{:S(2)}) async-start(bf16[32,16,512]{2,1,0:T(8,128)(2,1)} %bitcast.108), calls=%async_computation | async-start | bytes 1048576 | tf_op jit(solution)/shard_map/all_to_all | solution.py:76
  139.4 15.4 %copy-start = (f32[16,256,256]{2,1,0:T(8,128)S(1)}, f32[16,256,256]{2,1,0:T(8,128)}, u32[]{:S(2)}) copy-start(f32[16,256,256]{2,1,0:T(8,128)} %get-tuple-element.96) | copy-start | bytes 12582916
  139.5 15.4 %copy-start.1 = (bf16[16,64,256]{2,1,0:T(8,128)(2,1)S(1)}, bf16[16,64,256]{2,1,0:T(8,128)(2,1)}, u32[]{:S(2)}) copy-start(bf16[16,64,256]{2,1,0:T(8,128)(2,1)} %reshape.189) | copy-start | bytes 1572868
  183.0 0.8 copy-start.2
  186.2 5.8 %copy-start.13 = (f32[4096]{0:T(1024)S(1)}, f32[4096]{0:T(1024)}, u32[]{:S(2)}) copy-start(f32[4096]{0:T(1024)} %param.14) | copy-start | bytes 49156
  186.2 5.9 %copy-start.3 = (bf16[512,512]{0,1:T(8,128)(2,1)S(1)}, bf16[512,512]{0,1:T(8,128)(2,1)}, u32[]{:S(2)}) copy-start(bf16[512,512]{0,1:T(8,128)(2,1)} %copy-done.2) | copy-start | bytes 1572868
  186.2 55.7 %all-to-all-start.2 = ((bf16[8,512,512]{1,2,0:T(8,128)(2,1)}), bf16[8,512,512]{1,2,0:T(8,128)(2,1)}, u32[]{:S(2)}, u32[]{:S(2)}) async-start(bf16[8,512,512]{1,2,0:T(8,128)(2,1)} %stack.2), calls=%async_computation.2 | async-start | bytes 8388608 | tf_op jit(solution)/shard_map/all_to_all | solution.py:87
  256.9 15.6 %collective-permute-start.1 = (bf16[512,512]{1,0:T(8,128)(2,1)S(1)}, bf16[512,512]{1,0:T(8,128)(2,1)}, u32[]{:S(2)}, u32[]{:S(2)}) collective-permute-start(bf16[512,512]{1,0:T(8,128)(2,1)S(1)} %slice.119), channel_id=1, source_target_pairs={{0,8},{8,16},{16,24},{24,32},{32,40},{40,48},{48,56},{56,64},{64,7... | collective-permute-start | bytes 1572872 | tf_op jit(solution)/shard_map/ppermute | solution.py:18
  272.4 20.6 %collective-permute-start.2 = (bf16[512,512]{1,0:T(8,128)(2,1)}, bf16[512,512]{1,0:T(8,128)(2,1)}, u32[]{:S(2)}, u32[]{:S(2)}) collective-permute-start(bf16[512,512]{1,0:T(8,128)(2,1)} %collective-permute-done.1), channel_id=1, source_target_pairs={{0,8},{8,16},{16,24},{24,32},{32,40},{40,48},{48,56},{56,64},{64,7... | collective-permute-start | bytes 1572872 | tf_op jit(solution)/shard_map/ppermute | solution.py:18
  295.0 3.0 copy-start.4
  299.4 1.0 copy-start.6
Sparse Core Ops, SparseCore 0:
  12.7 73.2 all-gather.1
